TPU v7x, 256 devices: a whole 4x4x8 slice. The times are simulated.
256 devices in a mesh: lat: 16 (over x, y_hi, core), lon: 16 (over y_lo, z).
Axes of the slice: x: 4, y: 4 (y_hi: 2, y_lo: 2; y = y_hi * 2 + y_lo), z: 8, core: 2. Of those that a mesh axis runs over, the one named last changes fastest.
Arguments:
- feature: bfloat16 [512, 512, 384], P('lat', 'lon'), may hold values from -6 to 6
- coverage: int32 [512, 512], P('lat', 'lon'), may hold values 0 or 1
- band_rows: int32 [16], replicated, may hold values from 3 to 32, as said below
- depth_weight: bfloat16 [7, 7, 384], replicated, may hold values from -0.875 to 0.875
- norm_gain: float32 [384], replicated, may hold values from 0.25 to 1.75
- norm_shift: float32 [384], replicated, may hold values from -3 to 3
- up_weight: bfloat16 [384, 1536], P('lon'), may hold values from -0.3125 to 0.3125
- up_bias: float32 [1536], replicated, may hold values from -3 to 3
- down_weight: bfloat16 [1536, 384], P('lon'), may hold values from -0.15625 to 0.15625
- down_bias: float32 [384], replicated, may hold values from -3 to 3
- layer_scale: float32 [384], replicated, may hold values from 0.3 to 1.5
- cotangent: bfloat16 [512, 512, 384], P('lat', 'lon'), may hold values from -6 to 6
Outputs:
- block_out: bfloat16 [512, 512, 384], P('lat', 'lon')
- grad_in: bfloat16 [512, 512, 384], P('lat', 'lon')
- grad_up: float32 [384, 1536], P('lon')
- grad_down: float32 [1536, 384], P('lon')
- grad_depth: float32 [7, 7, 384], replicated
Inputs may be any that keep to these rules, and one draw needn't show every extreme that they name: `band_rows`: every band has 3 or more rows, the bands' rows sum to 256, and one band has exactly 32.
All inputs are finite; a program needn't handle non-finite values. No bound on the sum of `coverage` on one device may be relied on, other than what follows from the above.
Results may differ from a plain program's by a relative error of at most 0.0066.
Values may be sent and summed in bfloat16 or wider, within the bound.
A program may use at most 64 MiB of HBM per device.

v0:
```python
import math
import jax
import jax.numpy as jnp
from jax import lax
from jax.sharding import PartitionSpec as P

BAND_MEAN = 16
SQRT_TWO_PI = 0.7978845608028654
CUBIC = 0.044715
EPSILON = 1e-06


def padded(array, sides, width):
    for axis, dim in sides:
        size, length = (lax.axis_size(axis), array.shape[dim])
        up = [(i, (i + 1) % size) for i in range(size)]
        down = [(j, i) for i, j in up]
        last = lax.slice_in_dim(array, length - width, length, axis=dim)
        initial = lax.slice_in_dim(array, 0, width, axis=dim)
        before = lax.ppermute(last, axis, up)
        after = lax.ppermute(initial, axis, down)
        array = jnp.concatenate([before, array, after], axis=dim)
    return array


def shifted(block, axis, distance):
    devices = range(lax.axis_size(axis))
    route = [(i - distance, i) for i in devices if i - distance in devices]
    return lax.ppermute(block, axis, route)


def smooth_gate(pre_act):
    argument = SQRT_TWO_PI * (pre_act + CUBIC * pre_act * pre_act * pre_act)
    return 0.5 * pre_act * (1.0 + jnp.tanh(argument))


def smooth_slope(pre_act):
    argument = SQRT_TWO_PI * (pre_act + CUBIC * pre_act * pre_act * pre_act)
    tangent = jnp.tanh(argument)
    return 0.5 * (1.0 + tangent) + 0.5 * pre_act * (1.0 - tangent * tangent) * SQRT_TWO_PI * (
        1.0 + 3.0 * CUBIC * pre_act * pre_act
    )


def extend(field, live_rows):
    widened = padded(field, (("lon", 1),), 3)
    last_rows = lax.dynamic_slice_in_dim(widened, live_rows - 3, 3, 0)
    from_above = shifted(last_rows, "lat", 1)
    from_below = shifted(widened[:3], "lat", -1)
    zero_rows = jnp.zeros((3,) + widened.shape[1:], widened.dtype)
    stacked = jnp.concatenate([from_above, widened, zero_rows], axis=0)
    return lax.dynamic_update_slice_in_dim(stacked, from_below, live_rows + 3, 0)


def shards(
    feature,
    coverage,
    band_rows,
    depth_weight,
    norm_gain,
    norm_shift,
    up_weight,
    up_bias,
    down_weight,
    down_bias,
    layer_scale,
    cotangent,
):
    rows_max, tile_cols, channels = feature.shape
    kernel = depth_weight.shape[0]
    live_rows = lax.dynamic_index_in_dim(band_rows, lax.axis_index("lat"), 0, keepdims=False)
    inside = jnp.arange(rows_max, dtype=jnp.int32) < live_rows
    covered = jnp.where(inside[:, None], coverage, 0).astype(jnp.bfloat16)
    masked = feature * covered[:, :, None]
    framed = extend(masked, live_rows)
    depth_out = jnp.zeros((rows_max, tile_cols, channels), jnp.float32)
    for row_off in range(kernel):
        for col_off in range(kernel):
            depth_out = depth_out + framed[
                row_off : row_off + rows_max, col_off : col_off + tile_cols
            ].astype(jnp.float32) * depth_weight[row_off, col_off].astype(jnp.float32)
    full_up, full_down = (
        lax.all_gather(up_weight, "lon", axis=0, tiled=True),
        lax.all_gather(down_weight, "lon", axis=0, tiled=True),
    )
    depth_rows = depth_out.reshape(-1, channels)
    center = jnp.mean(depth_rows, axis=-1, keepdims=True)
    offset = depth_rows - center
    scale_inv = lax.rsqrt(jnp.mean(offset * offset, axis=-1, keepdims=True) + EPSILON)
    standard = offset * scale_inv
    normed = (standard * norm_gain + norm_shift).astype(jnp.bfloat16)
    before = jnp.dot(normed, full_up, preferred_element_type=jnp.float32) + up_bias
    active = smooth_gate(before).astype(jnp.bfloat16)
    branch = jnp.dot(active, full_down, preferred_element_type=jnp.float32) + down_bias
    result = (feature.reshape(-1, channels).astype(jnp.float32) + layer_scale * branch).astype(
        jnp.bfloat16
    )
    cot_live = jnp.where(inside[:, None, None], cotangent, jnp.zeros_like(cotangent)).reshape(
        -1, channels
    )
    upstream = (layer_scale * cot_live.astype(jnp.float32)).astype(jnp.bfloat16)
    sum_down = lax.dot_general(
        active, upstream, (((0,), (0,)), ((), ())), preferred_element_type=jnp.float32
    )
    back_active = lax.dot_general(
        upstream, full_down, (((1,), (1,)), ((), ())), preferred_element_type=jnp.float32
    )
    back_before = (back_active * smooth_slope(before)).astype(jnp.bfloat16)
    sum_up = lax.dot_general(
        normed, back_before, (((0,), (0,)), ((), ())), preferred_element_type=jnp.float32
    )
    back_normed = lax.dot_general(
        back_before, full_up, (((1,), (1,)), ((), ())), preferred_element_type=jnp.float32
    )
    back_unit = back_normed * norm_gain
    back_depth = scale_inv * (
        back_unit
        - jnp.mean(back_unit, axis=-1, keepdims=True)
        - standard * jnp.mean(back_unit * standard, axis=-1, keepdims=True)
    )
    back_depth = back_depth.astype(jnp.bfloat16).reshape(rows_max, tile_cols, channels)
    framed_back = extend(back_depth, live_rows)
    spread = jnp.zeros((rows_max, tile_cols, channels), jnp.float32)
    tap_list = []
    for row_off in range(kernel):
        for col_off in range(kernel):
            spread = spread + framed_back[
                6 - row_off : 6 - row_off + rows_max, 6 - col_off : 6 - col_off + tile_cols
            ].astype(jnp.float32) * depth_weight[row_off, col_off].astype(jnp.float32)
            tap_list.append(
                jnp.sum(
                    framed[row_off : row_off + rows_max, col_off : col_off + tile_cols].astype(
                        jnp.float32
                    )
                    * back_depth.astype(jnp.float32),
                    axis=(0, 1),
                )
            )
    grad_local = (
        cotangent.astype(jnp.float32) + covered.astype(jnp.float32)[:, :, None] * spread
    ).astype(jnp.bfloat16)
    grad_in = jnp.where(inside[:, None, None], grad_local, jnp.zeros_like(grad_local))
    block_out = jnp.where(
        inside[:, None, None],
        result.reshape(rows_max, tile_cols, channels),
        jnp.zeros_like(feature),
    )
    rscale = 1.0 / math.sqrt(BAND_MEAN * lax.axis_size("lat") * tile_cols * lax.axis_size("lon"))
    tap_terms = jnp.stack(tap_list, axis=0).reshape(kernel, kernel, channels)
    grad_depth = lax.psum(tap_terms, ("lat", "lon")) * rscale
    up_part, down_part = (
        lax.psum_scatter(sum_up, "lon", scatter_dimension=0, tiled=True),
        lax.psum_scatter(sum_down, "lon", scatter_dimension=0, tiled=True),
    )
    up_part, down_part = lax.psum((up_part, down_part), "lat")
    return (block_out, grad_in, up_part * rscale, down_part * rscale, grad_depth)


def solution(mesh):
    placed = (
        P("lat", "lon", None),
        P("lat", "lon"),
        P(),
        P(),
        P(),
        P(),
        P("lon", None),
        P(),
        P("lon", None),
        P(),
        P(),
        P("lat", "lon", None),
    )
    return jax.shard_map(
        shards,
        mesh=mesh,
        in_specs=placed,
        out_specs=(
            P("lat", "lon", None),
            P("lat", "lon", None),
            P("lon", None),
            P("lon", None),
            P(),
        ),
        check_vma=False,
    )
```

profile of v0, /device:TPU:8, one launch (start us, length us, event | category | flops | bytes accessed | tf_op | source)
XLA Modules:
  0.0 711.5 jit_solution(1951065629706237876)
XLA Ops:
  7.2 0.0 all-gather.3.cloned.1.call-start
  7.2 0.7 all-gather.3.cloned.1.call-update
  7.9 0.0 all-gather.5.cloned.1.call-start
  8.0 1.2 dynamic_slice.10
  9.2 0.6 iota_compare_fusion
  9.9 0.8 fusion.108
  10.7 1.3 broadcast_multiply_fusion
  12.0 0.1 fusion.114
  12.1 2.0 collective-permute-start
  14.1 3.9 collective-permute-start.1
  18.0 0.0 all-gather.5.cloned.1.call-update
  18.0 0.0 all-reduce.4.cloned.1.call-start
  20.7 0.1 convert_reduce_fusion.47
  21.0 0.7 pad.12.clone
  21.7 0.1 convert_reduce_fusion.48
  22.0 0.6 pad_maximum_fusion
  22.6 1.5 collective-permute-start.2
  24.0 0.7 convert_reduce_fusion.46
  24.7 1.3 collective-permute-start.3
  26.0 1.1 maximum_maximum_fusion
  27.1 3.4 collective-permute-done.3
  30.9 12.5 %fusion.109 = (f32[32,32]{1,0:T(8,128)S(1)}, f32[32,32,384]{2,1,0:T(8,128)S(1)}) fusion(f32[384]{0:T(512)} %get-tuple-element.103, bf16[38,38,384]{2,1,0:T(8,128)(2,1)S(1)} %constant_dynamic-update-slice_fusion.1, f32[384]{0:T(512)} %get-tuple-element.104, f32[384]{0:T(512)S(1)} %get-tuple-element.57, f32[384]{0:T(512)S(1)} %get-tuple-element.58, ...), kind=kLoop, calls=%fused_computation.289 | loop fusion | flops 57801728 | bytes 40187392 | tf_op jit(solution)/shard_map/reduce_sum | solution.py:87
  43.5 0.1 div.15
  43.6 0.4 multiply_reduce_fusion.1
  44.0 0.1 rsqrt.12
  44.0 0.1 copy-done.87
  44.2 1.2 add_convert_fusion.1
  45.4 36.1 %all-gather.3.cloned.1.call-done = bf16[384,1536]{1,0:T(8,128)(2,1)} async-done(((bf16[24,1536]{1,0:T(8,128)(2,1)}), bf16[384,1536]{1,0:T(8,128)(2,1)}) %all-gather.3.cloned.1.call-update) | async-done | bytes 1179664 | tf_op jit(solution)/shard_map/all_gather | solution.py:83
  81.5 7.8 %multiply_convert_fusion = (bf16[1024,1536]{1,0:T(8,128)(2,1)}, f32[1024,1536]{1,0:T(8,128)}) fusion(f32[1536]{0:T(1024)} %param.19, bf16[1024,384]{1,0:T(8,128)(2,1)} %add_convert_fusion.1, bf16[384,1536]{1,0:T(8,128)(2,1)} %all-gather.3.cloned.1.call-done), kind=kOutput, calls=%fused_computation.58 | convolution fusion | flops 1223688192 | bytes 11409408 | tf_op jit(solution)/shard_map/dot_general | solution.py:92
  89.3 61.2 %all-gather.5.cloned.1.call-done = bf16[1536,384]{1,0:T(8,128)(2,1)} async-done(((bf16[96,384]{1,0:T(8,128)(2,1)}), bf16[1536,384]{1,0:T(8,128)(2,1)}) %all-gather.5.cloned.1.call-update) | async-done | bytes 1179664 | tf_op jit(solution)/shard_map/all_gather | solution.py:84
  150.5 4.2 fusion.105
  154.7 1.1 broadcast_select_fusion.1
  155.8 0.2 fusion.104
  156.1 1.2 copy-done.92
  157.3 5.4 fusion.6
  162.7 2.0 fusion.107
  164.8 5.0 fusion.103
  169.7 3.0 fusion.67
  172.8 4.0 fusion.85
  177.3 0.2 stack.199
  177.5 0.7 reshape.86
  178.2 0.0 reduce-scatter.5.cloned.1.call-start
  178.2 5.2 fusion.116
  183.4 0.0 reduce-scatter.3.cloned.1.call-start
  183.5 1.1 copy-done.5
  184.6 4.7 fusion.115
  189.3 0.0 all-reduce.6.cloned.1.call-start
  189.3 0.1 fusion.113
  189.4 0.7 collective-permute-start.4
  190.1 3.5 collective-permute-start.5
  193.6 2.6 collective-permute-done.4
  196.3 0.6 pad_maximum_fusion.1
  197.2 1.3 collective-permute-start.6
  198.5 218.1 %all-reduce.4.cloned.1.call-done = f32[7,7,384]{2,1,0:T(8,128)} async-done(((f32[7,7,384]{2,1,0:T(8,128)}), f32[7,7,384]{2,1,0:T(8,128)}) %all-reduce.4.cloned.1.call-update) | async-done | bytes 75280 | tf_op jit(solution)/shard_map/psum | solution.py:150
  416.6 1.5 broadcast_multiply_fusion.3
  418.1 1.3 collective-permute-start.7
  419.4 1.1 maximum_maximum_fusion.1
  420.5 0.8 collective-permute-done.7
  421.3 68.6 %reduce-scatter.5.cloned.1.call-done = f32[96,384]{1,0:T(8,128)} async-done(((f32[1536,384]{1,0:T(8,128)}), f32[96,384]{1,0:T(8,128)}) %reduce-scatter.5.cloned.1.call-update) | async-done | bytes 147472 | tf_op jit(solution)/shard_map/reduce_scatter | solution.py:153
  489.9 73.4 %reduce-scatter.3.cloned.1.call-done = f32[24,1536]{1,0:T(8,128)} async-done(((f32[384,1536]{1,0:T(8,128)}), f32[24,1536]{1,0:T(8,128)}) %reduce-scatter.3.cloned.1.call-update) | async-done | bytes 147472 | tf_op jit(solution)/shard_map/reduce_scatter | solution.py:152
  563.8 12.6 %broadcast_select_fusion = bf16[32,32,384]{2,1,0:T(8,128)(2,1)} fusion(pred[32]{0:T(512)(128)(4,1)} %copy-done.85, f32[384]{0:T(512)} %get-tuple-element.103, bf16[38,38,384]{2,1,0:T(8,128)(2,1)S(1)} %constant_dynamic-update-slice_fusion, f32[384]{0:T(512)} %get-tuple-element.104, f32[384]{0:T(512)S(1)} %copy-done.46, f32[384]{0:T(512)S(1)} %copy-done.48, ...), kind=kLoop, calls=%fused_computation.221 | loop fusion | flops 59375616 | bytes 40187424 | tf_op jit(solution)/shard_map/jit(_where)/select_n | solution.py:142
  576.3 125.2 %all-reduce.6.cloned.1.call-done = (f32[24,1536]{1,0:T(8,128)}, f32[96,384]{1,0:T(8,128)}) async-done(((f32[24,1536]{1,0:T(8,128)}, f32[96,384]{1,0:T(8,128)}), (f32[24,1536]{1,0:T(8,128)}, f32[96,384]{1,0:T(8,128)})) %all-reduce.6.cloned.1.call-update) | async-done | bytes 294928 | tf_op jit(solution)/shard_map/psum | solution.py:155
  701.5 1.6 broadcast_multiply_fusion.2
  703.1 1.6 broadcast_multiply_fusion.1
  (255 shorter events, 0.8 us)
Async XLA Ops:
  7.2 13.5 %copy-start.6 = (bf16[7,7,384]{2,1,0:T(8,128)(2,1)S(1)}, bf16[7,7,384]{2,1,0:T(8,128)(2,1)}, u32[]{:S(2)}) copy-start(bf16[7,7,384]{2,1,0:T(8,128)(2,1)} %param.15) | copy-start | bytes 112900
  7.2 74.3 %all-gather.3.cloned.1.call-start = ((), (), s32[]{:S(2)}) async-start(), calls=%async_computation.2 | async-start | bytes 1253376 | tf_op jit(solution)/shard_map/all_gather | solution.py:83
  7.9 142.6 %all-gather.5.cloned.1.call-start = ((), (), s32[]{:S(2)}) async-start(), calls=%async_computation.3 | async-start | bytes 1253376 | tf_op jit(solution)/shard_map/all_gather | solution.py:84
  12.1 9.8 %collective-permute-start = (bf16[32,3,384]{2,1,0:T(4,128)(2,1)S(1)}, bf16[32,3,384]{2,1,0:T(4,128)(2,1)S(1)}, u32[]{:S(2)}, u32[]{:S(2)}) collective-permute-start(bf16[32,3,384]{2,1,0:T(4,128)(2,1)S(1)} %get-tuple-element.118), channel_id=1, source_target_pairs={{0,1},{1,2},{2,3},{3,4},{4,5},{5,6},{6,7},{7,8},{8,9},{9,10},{10,1... | collective-permute-start | bytes 221192 | tf_op jit(solution)/shard_map/ppermute | solution.py:20
  14.1 7.9 %collective-permute-start.1 = (bf16[32,3,384]{2,1,0:T(4,128)(2,1)S(1)}, bf16[32,3,384]{2,1,0:T(4,128)(2,1)S(1)}, u32[]{:S(2)}, u32[]{:S(2)}) collective-permute-start(bf16[32,3,384]{2,1,0:T(4,128)(2,1)S(1)} %get-tuple-element.119), channel_id=1, source_target_pairs={{1,0},{2,1},{3,2},{4,3},{5,4},{6,5},{7,6},{8,7},{9,8},{10,9},{11,1... | collective-permute-start | bytes 221192 | tf_op jit(solution)/shard_map/ppermute | solution.py:21
  18.0 398.6 %all-reduce.4.cloned.1.call-start = ((), (), s32[]{:S(2)}) async-start(), calls=%async_computation.6 | async-start | bytes 172032 | tf_op jit(solution)/shard_map/psum | solution.py:150
  20.8 9.8 %copy-start.9 = (f32[384]{0:T(512)}, f32[384]{0:T(512)S(1)}, u32[]{:S(2)}) copy-start(f32[384]{0:T(512)S(1)} %get-tuple-element.77) | copy-start | bytes 4612
  20.8 9.8 %copy-start.11 = (f32[384]{0:T(512)}, f32[384]{0:T(512)S(1)}, u32[]{:S(2)}) copy-start(f32[384]{0:T(512)S(1)} %get-tuple-element.78) | copy-start | bytes 4612
  20.8 9.8 %copy-start.13 = (f32[384]{0:T(512)}, f32[384]{0:T(512)S(1)}, u32[]{:S(2)}) copy-start(f32[384]{0:T(512)S(1)} %get-tuple-element.79) | copy-start | bytes 4612
  20.8 9.8 %copy-start.15 = (f32[384]{0:T(512)}, f32[384]{0:T(512)S(1)}, u32[]{:S(2)}) copy-start(f32[384]{0:T(512)S(1)} %get-tuple-element.80) | copy-start | bytes 4612
  20.8 9.8 %copy-start.17 = (f32[384]{0:T(512)}, f32[384]{0:T(512)S(1)}, u32[]{:S(2)}) copy-start(f32[384]{0:T(512)S(1)} %get-tuple-element.81) | copy-start | bytes 4612
  20.8 9.8 %copy-start.19 = (f32[384]{0:T(512)}, f32[384]{0:T(512)S(1)}, u32[]{:S(2)}) copy-start(f32[384]{0:T(512)S(1)} %get-tuple-element.82) | copy-start | bytes 4612
  22.6 3.4 collective-permute-start.2
  24.7 18.8 %copy-start.81 = (f32[384]{0:T(512)}, f32[384]{0:T(512)S(1)}, u32[]{:S(2)}) copy-start(f32[384]{0:T(512)S(1)} %get-tuple-element.94) | copy-start | bytes 4612
  24.7 18.8 %copy-start.83 = (f32[384]{0:T(512)}, f32[384]{0:T(512)S(1)}, u32[]{:S(2)}) copy-start(f32[384]{0:T(512)S(1)} %get-tuple-element.95) | copy-start | bytes 4612
  24.7 5.8 collective-permute-start.3
  45.4 105.1 %copy-start.2 = (bf16[32,32,384]{2,1,0:T(8,128)(2,1)S(1)}, bf16[32,32,384]{2,1,0:T(8,128)(2,1)}, u32[]{:S(2)}) copy-start(bf16[32,32,384]{2,1,0:T(8,128)(2,1)} %param.12) | copy-start | bytes 2359300
  178.2 311.8 %reduce-scatter.5.cloned.1.call-start = ((), (), s32[]{:S(2)}) async-start(), calls=%async_computation.5 | async-start | bytes 2506752 | tf_op jit(solution)/shard_map/reduce_scatter | solution.py:153
  183.4 379.9 %reduce-scatter.3.cloned.1.call-start = ((), (), s32[]{:S(2)}) async-start(), calls=%async_computation.4 | async-start | bytes 2506752 | tf_op jit(solution)/shard_map/reduce_scatter | solution.py:152
  189.3 512.2 %all-reduce.6.cloned.1.call-start = ((), (), s32[]{:S(2)}) async-start(), calls=%async_computation.7 | async-start | bytes 589824 | tf_op jit(solution)/shard_map/psum | solution.py:155
  189.4 6.8 collective-permute-start.4
  190.1 6.1 collective-permute-start.5
  196.8 366.5 %copy-start.1 = (bf16[32,32,384]{2,1,0:T(8,128)(2,1)S(1)}, bf16[32,32,384]{2,1,0:T(8,128)(2,1)}, u32[]{:S(2)}) copy-start(bf16[32,32,384]{2,1,0:T(8,128)(2,1)} %param.23) | copy-start | bytes 2359300
  196.8 366.5 %copy-start.8 = (f32[384]{0:T(512)S(1)}, f32[384]{0:T(512)}, u32[]{:S(2)}) copy-start(f32[384]{0:T(512)} %copy-done.7) | copy-start | bytes 4612
  196.8 366.5 %copy-start.10 = (f32[384]{0:T(512)S(1)}, f32[384]{0:T(512)}, u32[]{:S(2)}) copy-start(f32[384]{0:T(512)} %copy-done.9) | copy-start | bytes 4612
  196.8 366.5 %copy-start.12 = (f32[384]{0:T(512)S(1)}, f32[384]{0:T(512)}, u32[]{:S(2)}) copy-start(f32[384]{0:T(512)} %copy-done.11) | copy-start | bytes 4612
  196.9 366.5 %copy-start.14 = (f32[384]{0:T(512)S(1)}, f32[384]{0:T(512)}, u32[]{:S(2)}) copy-start(f32[384]{0:T(512)} %copy-done.13) | copy-start | bytes 4612
  196.9 366.5 %copy-start.16 = (f32[384]{0:T(512)S(1)}, f32[384]{0:T(512)}, u32[]{:S(2)}) copy-start(f32[384]{0:T(512)} %copy-done.15) | copy-start | bytes 4612
  196.9 366.5 %copy-start.18 = (f32[384]{0:T(512)S(1)}, f32[384]{0:T(512)}, u32[]{:S(2)}) copy-start(f32[384]{0:T(512)} %copy-done.17) | copy-start | bytes 4612
  196.9 366.5 %copy-start.20 = (f32[384]{0:T(512)S(1)}, f32[384]{0:T(512)}, u32[]{:S(2)}) copy-start(f32[384]{0:T(512)} %copy-done.19) | copy-start | bytes 4612
  196.9 366.5 %copy-start.22 = (f32[384]{0:T(512)S(1)}, f32[384]{0:T(512)}, u32[]{:S(2)}) copy-start(f32[384]{0:T(512)} %copy-done.21) | copy-start | bytes 4612
  196.9 366.5 %copy-start.24 = (f32[384]{0:T(512)S(1)}, f32[384]{0:T(512)}, u32[]{:S(2)}) copy-start(f32[384]{0:T(512)} %copy-done.23) | copy-start | bytes 4612
  196.9 366.5 %copy-start.26 = (f32[384]{0:T(512)S(1)}, f32[384]{0:T(512)}, u32[]{:S(2)}) copy-start(f32[384]{0:T(512)} %copy-done.25) | copy-start | bytes 4612
  196.9 366.5 %copy-start.28 = (f32[384]{0:T(512)S(1)}, f32[384]{0:T(512)}, u32[]{:S(2)}) copy-start(f32[384]{0:T(512)} %copy-done.27) | copy-start | bytes 4612
  196.9 366.5 %copy-start.30 = (f32[384]{0:T(512)S(1)}, f32[384]{0:T(512)}, u32[]{:S(2)}) copy-start(f32[384]{0:T(512)} %copy-done.29) | copy-start | bytes 4612
  196.9 366.5 %copy-start.32 = (f32[384]{0:T(512)S(1)}, f32[384]{0:T(512)}, u32[]{:S(2)}) copy-start(f32[384]{0:T(512)} %copy-done.31) | copy-start | bytes 4612
  197.0 366.5 %copy-start.34 = (f32[384]{0:T(512)S(1)}, f32[384]{0:T(512)}, u32[]{:S(2)}) copy-start(f32[384]{0:T(512)} %copy-done.33) | copy-start | bytes 4612
  197.0 366.5 %copy-start.36 = (f32[384]{0:T(512)S(1)}, f32[384]{0:T(512)}, u32[]{:S(2)}) copy-start(f32[384]{0:T(512)} %copy-done.35) | copy-start | bytes 4612
  197.0 366.5 %copy-start.38 = (f32[384]{0:T(512)S(1)}, f32[384]{0:T(512)}, u32[]{:S(2)}) copy-start(f32[384]{0:T(512)} %copy-done.37) | copy-start | bytes 4612
  197.0 366.5 %copy-start.40 = (f32[384]{0:T(512)S(1)}, f32[384]{0:T(512)}, u32[]{:S(2)}) copy-start(f32[384]{0:T(512)} %copy-done.39) | copy-start | bytes 4612
  197.0 366.5 %copy-start.42 = (f32[384]{0:T(512)S(1)}, f32[384]{0:T(512)}, u32[]{:S(2)}) copy-start(f32[384]{0:T(512)} %copy-done.41) | copy-start | bytes 4612
  197.0 366.5 %copy-start.44 = (f32[384]{0:T(512)S(1)}, f32[384]{0:T(512)}, u32[]{:S(2)}) copy-start(f32[384]{0:T(512)} %copy-done.43) | copy-start | bytes 4612
  197.0 366.5 %copy-start.46 = (f32[384]{0:T(512)S(1)}, f32[384]{0:T(512)}, u32[]{:S(2)}) copy-start(f32[384]{0:T(512)} %copy-done.45) | copy-start | bytes 4612
  197.0 366.5 %copy-start.48 = (f32[384]{0:T(512)S(1)}, f32[384]{0:T(512)}, u32[]{:S(2)}) copy-start(f32[384]{0:T(512)} %copy-done.47) | copy-start | bytes 4612
  197.0 366.5 %copy-start.50 = (f32[384]{0:T(512)S(1)}, f32[384]{0:T(512)}, u32[]{:S(2)}) copy-start(f32[384]{0:T(512)} %copy-done.49) | copy-start | bytes 4612
  197.0 366.5 %copy-start.52 = (f32[384]{0:T(512)S(1)}, f32[384]{0:T(512)}, u32[]{:S(2)}) copy-start(f32[384]{0:T(512)} %copy-done.51) | copy-start | bytes 4612
  197.1 366.5 %copy-start.54 = (f32[384]{0:T(512)S(1)}, f32[384]{0:T(512)}, u32[]{:S(2)}) copy-start(f32[384]{0:T(512)} %copy-done.53) | copy-start | bytes 4612
  197.1 366.5 %copy-start.56 = (f32[384]{0:T(512)S(1)}, f32[384]{0:T(512)}, u32[]{:S(2)}) copy-start(f32[384]{0:T(512)} %copy-done.55) | copy-start | bytes 4612
  197.1 366.5 %copy-start.58 = (f32[384]{0:T(512)S(1)}, f32[384]{0:T(512)}, u32[]{:S(2)}) copy-start(f32[384]{0:T(512)} %copy-done.57) | copy-start | bytes 4612
  197.1 366.5 %copy-start.60 = (f32[384]{0:T(512)S(1)}, f32[384]{0:T(512)}, u32[]{:S(2)}) copy-start(f32[384]{0:T(512)} %copy-done.59) | copy-start | bytes 4612
  197.1 366.5 %copy-start.62 = (f32[384]{0:T(512)S(1)}, f32[384]{0:T(512)}, u32[]{:S(2)}) copy-start(f32[384]{0:T(512)} %copy-done.61) | copy-start | bytes 4612
  197.1 366.5 %copy-start.64 = (f32[384]{0:T(512)S(1)}, f32[384]{0:T(512)}, u32[]{:S(2)}) copy-start(f32[384]{0:T(512)} %copy-done.63) | copy-start | bytes 4612
  197.1 366.5 %copy-start.66 = (f32[384]{0:T(512)S(1)}, f32[384]{0:T(512)}, u32[]{:S(2)}) copy-start(f32[384]{0:T(512)} %copy-done.65) | copy-start | bytes 4612
  197.1 366.5 %copy-start.68 = (f32[384]{0:T(512)S(1)}, f32[384]{0:T(512)}, u32[]{:S(2)}) copy-start(f32[384]{0:T(512)} %copy-done.67) | copy-start | bytes 4612
  197.1 366.5 %copy-start.70 = (f32[384]{0:T(512)S(1)}, f32[384]{0:T(512)}, u32[]{:S(2)}) copy-start(f32[384]{0:T(512)} %copy-done.69) | copy-start | bytes 4612
  197.1 366.5 %copy-start.72 = (f32[384]{0:T(512)S(1)}, f32[384]{0:T(512)}, u32[]{:S(2)}) copy-start(f32[384]{0:T(512)} %copy-done.71) | copy-start | bytes 4612
  197.2 366.5 %copy-start.74 = (f32[384]{0:T(512)S(1)}, f32[384]{0:T(512)}, u32[]{:S(2)}) copy-start(f32[384]{0:T(512)} %copy-done.73) | copy-start | bytes 4612
  197.2 366.5 %copy-start.76 = (f32[384]{0:T(512)S(1)}, f32[384]{0:T(512)}, u32[]{:S(2)}) copy-start(f32[384]{0:T(512)} %copy-done.75) | copy-start | bytes 4612
  197.2 366.5 %copy-start.78 = (f32[384]{0:T(512)S(1)}, f32[384]{0:T(512)}, u32[]{:S(2)}) copy-start(f32[384]{0:T(512)} %copy-done.77) | copy-start | bytes 4612
  197.2 366.5 %copy-start.80 = (f32[384]{0:T(512)S(1)}, f32[384]{0:T(512)}, u32[]{:S(2)}) copy-start(f32[384]{0:T(512)} %copy-done.79) | copy-start | bytes 4612
  197.2 366.5 %copy-start.82 = (f32[384]{0:T(512)S(1)}, f32[384]{0:T(512)}, u32[]{:S(2)}) copy-start(f32[384]{0:T(512)} %copy-done.81) | copy-start | bytes 4612
  197.2 366.5 %copy-start.84 = (f32[384]{0:T(512)S(1)}, f32[384]{0:T(512)}, u32[]{:S(2)}) copy-start(f32[384]{0:T(512)} %copy-done.83) | copy-start | bytes 4612
  197.2 222.2 %collective-permute-start.6 = (bf16[3,38,384]{2,1,0:T(8,128)(2,1)S(1)}, bf16[3,38,384]{2,1,0:T(8,128)(2,1)S(1)}, u32[]{:S(2)}, u32[]{:S(2)}) collective-permute-start(bf16[3,38,384]{2,1,0:T(8,128)(2,1)S(1)} %get-tuple-element.113), channel_id=1, source_target_pairs={{0,16},{16,32},{32,48},{48,64},{64,80},{80,96},{96,112},{112,128},... | collective-permute-start | bytes 262664 | tf_op jit(solution)/shard_map/ppermute | solution.py:29
  418.1 3.2 collective-permute-start.7
  (46 other events, 333.8 us)
Sparse Core Ops, SparseCore 0:
  9.8 71.6 all-gather.2
  83.3 67.1 all-gather.4
  178.3 238.2 all-reduce.3
  419.0 70.8 reduce-scatter.4
  492.3 70.9 reduce-scatter.2
  565.9 135.5 all-reduce.5
where the time goes:
time: 712 us
  waiting for transfers between devices  590 us (83%)
  other arithmetic  51.7 us (7%)
  matrix products  29.3 us (4%)
  between operations  18.7 us (3%)
  starting transfers between devices  15.7 us (2%)
    psum x1, waiting for transfers between devices, shards(): grad_depth = lax.psum(tap_terms, ('lat', 'lon')) * rscale  218 us
    psum x1, waiting for transfers between devices, shards(): up_part, down_part = lax.psum((up_part, down_part), 'lat')  125 us
    reduce_scatter x1, waiting for transfers between devices, shards(): lax.psum_scatter(sum_up, 'lon', scatter_dimension=0, tiled=True)  73.4 us
    reduce_scatter x1, waiting for transfers between devices, shards(): lax.psum_scatter(sum_down, 'lon', scatter_dimension=0, tiled=True)  68.6 us
    all_gather x1, waiting for transfers between devices, shards(): lax.all_gather(down_weight, 'lon', axis=0, tiled=True)  61.2 us
    all_gather x1, waiting for transfers between devices, shards(): lax.all_gather(up_weight, 'lon', axis=0, tiled=True)  36.1 us
  transfers between devices with their start and end apart: 14, of which 9 were waited for; matrix products, arithmetic and copies ran while one was open for 8% of the time, Pallas kernels for 0%

commit v1 on v0

--- a/solution.py
+++ b/solution.py
@@ -147,7 +147,7 @@
     )
     rscale = 1.0 / math.sqrt(BAND_MEAN * lax.axis_size("lat") * tile_cols * lax.axis_size("lon"))
     tap_terms = jnp.stack(tap_list, axis=0).reshape(kernel, kernel, channels)
-    grad_depth = lax.psum(tap_terms, ("lat", "lon")) * rscale
+    grad_depth = lax.psum(lax.psum(tap_terms, "lat"), "lon") * rscale
     up_part, down_part = (
         lax.psum_scatter(sum_up, "lon", scatter_dimension=0, tiled=True),
         lax.psum_scatter(sum_down, "lon", scatter_dimension=0, tiled=True),

time: 712 us -> 592 us (0.83)
  waiting for transfers between devices: 590 us -> 470 us
    psum x1, waiting for transfers between devices: 218 us -> 129 us  [shards(): grad_depth = lax.psum(lax.psum(tap_terms, 'lat'), 'lon') * rscale]
    reduce_scatter x1, waiting for transfers between devices: 68.6 us -> 30.6 us  [shards(): lax.psum_scatter(sum_down, 'lon', scatter_dimension=0, tiled=True)]
  transfers between devices with their start and end apart: 14 -> 14, of which waited for: 9 -> 8; matrix products, arithmetic and copies ran while one was open for 8% -> 12% of each run, Pallas kernels for 0% -> 0%
where the time goes in v1:
time: 592 us; the launch traced here: 591 us
  waiting for transfers between devices  470 us (79%)
  other arithmetic  49.5 us (8%)
  matrix products  29.4 us (5%)
  between operations  18.8 us (3%)
  starting transfers between devices  16.4 us (3%)
  local copies, waits for them, and re-layouts  6.35 us (1%)
    psum x1, waiting for transfers between devices, shards(): up_part, down_part = lax.psum((up_part, down_part), 'lat')  131 us
    psum x1, waiting for transfers between devices, shards(): grad_depth = lax.psum(lax.psum(tap_terms, 'lat'), 'lon') * rscale  129 us
    reduce_scatter x1, waiting for transfers between devices, shards(): lax.psum_scatter(sum_up, 'lon', scatter_dimension=0, tiled=True)  73.5 us
    all_gather x1, waiting for transfers between devices, shards(): lax.all_gather(down_weight, 'lon', axis=0, tiled=True)  61.2 us
    all_gather x1, waiting for transfers between devices, shards(): lax.all_gather(up_weight, 'lon', axis=0, tiled=True)  37.6 us
    reduce_scatter x1, waiting for transfers between devices, shards(): lax.psum_scatter(sum_down, 'lon', scatter_dimension=0, tiled=True)  30.6 us
    select_n x1, other arithmetic, shards(): jnp.where(inside[:, None, None], grad_local, jnp.zeros_like(grad_local))  12.3 us
  transfers between devices with their start and end apart: 14, of which 8 were waited for; matrix products, arithmetic and copies ran while one was open for 12% of the time, Pallas kernels for 0%

profile of v1, /device:TPU:8, one launch (start us, length us, event | category | flops | bytes accessed | tf_op | source)
XLA Modules:
  0.0 590.6 jit_solution(18299306006039303611)
XLA Ops:
  7.2 0.0 all-gather.3.cloned.1.call-start
  7.2 0.7 all-gather.3.cloned.1.call-update
  7.9 0.0 all-gather.5.cloned.1.call-start
  8.0 1.2 dynamic_slice.10
  9.2 0.6 iota_compare_fusion
  9.9 0.8 fusion.108
  10.7 1.3 broadcast_multiply_fusion
  12.0 0.1 fusion.114
  12.1 2.0 collective-permute-start
  14.1 3.9 collective-permute-start.1
  18.0 0.0 all-gather.5.cloned.1.call-update
  18.0 0.0 reduce-scatter.5.cloned.1.call-start
  20.7 0.7 convert_reduce_fusion.47
  21.4 0.1 pad.12.clone
  21.5 0.1 convert_reduce_fusion.48
  21.8 0.6 pad_maximum_fusion
  22.5 1.5 collective-permute-start.2
  24.0 0.1 convert_reduce_fusion.46
  24.2 1.5 collective-permute-start.3
  25.7 0.4 maximum_maximum_fusion
  26.1 3.9 collective-permute-done.3
  30.4 11.6 %fusion.109 = (f32[32,32]{1,0:T(8,128)S(1)}, f32[32,32,384]{2,1,0:T(8,128)S(1)}) fusion(f32[384]{0:T(512)S(1)} %get-tuple-element.103, bf16[38,38,384]{2,1,0:T(8,128)(2,1)S(1)} %constant_dynamic-update-slice_fusion.1, f32[384]{0:T(512)S(1)} %get-tuple-element.104, f32[384]{0:T(512)S(1)} %get-tuple-element.57, f32[384]{0:T(512)S(1)} %get-tuple-element.58, ...), kind=kLoop, calls=%fused_computation.289 | loop fusion | flops 57801728 | bytes 40187392 | tf_op jit(solution)/shard_map/reduce_sum | solution.py:87
  42.1 0.1 div.15
  42.2 0.4 multiply_reduce_fusion.1
  42.6 0.1 rsqrt.12
  42.6 0.1 copy-done.94
  42.8 1.2 add_convert_fusion.1
  44.0 37.6 %all-gather.3.cloned.1.call-done = bf16[384,1536]{1,0:T(8,128)(2,1)} async-done(((bf16[24,1536]{1,0:T(8,128)(2,1)}), bf16[384,1536]{1,0:T(8,128)(2,1)}) %all-gather.3.cloned.1.call-update) | async-done | bytes 1179664 | tf_op jit(solution)/shard_map/all_gather | solution.py:83
  81.6 7.8 %multiply_convert_fusion = (bf16[1024,1536]{1,0:T(8,128)(2,1)}, f32[1024,1536]{1,0:T(8,128)}) fusion(f32[1536]{0:T(1024)} %param.19, bf16[1024,384]{1,0:T(8,128)(2,1)} %add_convert_fusion.1, bf16[384,1536]{1,0:T(8,128)(2,1)} %all-gather.3.cloned.1.call-done), kind=kOutput, calls=%fused_computation.58 | convolution fusion | flops 1223688192 | bytes 11409408 | tf_op jit(solution)/shard_map/dot_general | solution.py:92
  89.4 61.2 %all-gather.5.cloned.1.call-done = bf16[1536,384]{1,0:T(8,128)(2,1)} async-done(((bf16[96,384]{1,0:T(8,128)(2,1)}), bf16[1536,384]{1,0:T(8,128)(2,1)}) %all-gather.5.cloned.1.call-update) | async-done | bytes 1179664 | tf_op jit(solution)/shard_map/all_gather | solution.py:84
  150.6 4.1 fusion.105
  154.7 1.1 broadcast_select_fusion.1
  155.9 0.2 fusion.104
  156.1 0.8 copy-done.100
  156.9 3.3 fusion.116
  160.2 0.3 reduce-scatter.3.cloned.1.call-start
  160.5 7.1 %fusion.6 = bf16[1024,1536]{1,0:T(8,128)(2,1)S(1)} fusion(f32[1024,1536]{1,0:T(8,128)} %get-tuple-element.124, bf16[1024,384]{1,0:T(8,128)(2,1)S(1)} %fusion.104, bf16[1536,384]{1,0:T(8,128)(2,1)} %all-gather.5.cloned.1.call-done, f32[1536]{0:T(1024)} %param.19), kind=kOutput, calls=%fused_computation.57 | convolution fusion | flops 1239416832 | bytes 11409408 | tf_op jit(solution)/shard_map/dot_general | solution.py:105
  167.7 1.7 copy-done.99
  169.3 2.9 fusion.115
  172.2 0.0 all-reduce.6.cloned.1.call-start
  172.2 0.6 copy-done.97
  172.8 4.2 fusion.107
  177.0 5.0 fusion.103
  182.0 0.1 fusion.113
  182.1 0.7 collective-permute-start.4
  182.8 3.5 collective-permute-start.5
  186.3 3.9 fusion.85
  190.3 0.6 pad_maximum_fusion.1
  190.8 1.3 collective-permute-start.6
  192.2 2.8 fusion.67
  195.9 0.2 stack.199
  196.1 0.7 reshape.86
  196.8 1.5 collective-permute-start.7
  198.3 1.1 maximum_maximum_fusion.1
  199.4 3.1 collective-permute-done.7
  202.5 30.6 %reduce-scatter.5.cloned.1.call-done = f32[96,384]{1,0:T(8,128)} async-done(((f32[1536,384]{1,0:T(8,128)}), f32[96,384]{1,0:T(8,128)}) %reduce-scatter.5.cloned.1.call-update) | async-done | bytes 147472 | tf_op jit(solution)/shard_map/reduce_scatter | solution.py:153
  233.1 73.5 %reduce-scatter.3.cloned.1.call-done = f32[24,1536]{1,0:T(8,128)} async-done(((f32[384,1536]{1,0:T(8,128)}), f32[24,1536]{1,0:T(8,128)}) %reduce-scatter.3.cloned.1.call-update) | async-done | bytes 147472 | tf_op jit(solution)/shard_map/reduce_scatter | solution.py:152
  306.6 0.0 all-reduce.4.cloned.1.call-start
  307.0 12.3 %broadcast_select_fusion = bf16[32,32,384]{2,1,0:T(8,128)(2,1)} fusion(pred[32]{0:T(512)(128)(4,1)} %copy-done.92, f32[384]{0:T(512)} %copy-done.90, bf16[38,38,384]{2,1,0:T(8,128)(2,1)S(1)} %constant_dynamic-update-slice_fusion, f32[384]{0:T(512)} %copy-done.91, f32[384]{0:T(512)S(1)} %copy-done.44, f32[384]{0:T(512)S(1)} %copy-done.46, ...), kind=kLoop, calls=%fused_computation.221 | loop fusion | flops 59375616 | bytes 40187424 | tf_op jit(solution)/shard_map/jit(_where)/select_n | solution.py:142
  319.4 130.9 %all-reduce.6.cloned.1.call-done = (f32[24,1536]{1,0:T(8,128)}, f32[96,384]{1,0:T(8,128)}, f32[7,7,384]{2,1,0:T(8,128)}) async-done(((f32[24,1536]{1,0:T(8,128)}, f32[96,384]{1,0:T(8,128)}, f32[7,7,384]{2,1,0:T(8,128)}), (f32[24,1536]{1,0:T(8,128)}, f32[96,384]{1,0:T(8,128)}, f32[7,7,384]{2,1,0:T(8,128)})) %all-reduce.6.cloned.1.call-update) | async-done | bytes 370192 | tf_op jit(solution)/shard_map/psum | solution.py:155
  450.3 1.6 broadcast_multiply_fusion.2
  451.9 1.6 broadcast_multiply_fusion.1
  453.4 128.8 %all-reduce.4.cloned.1.call-done = f32[7,7,384]{2,1,0:T(8,128)} async-done(((f32[7,7,384]{2,1,0:T(8,128)}), f32[7,7,384]{2,1,0:T(8,128)}) %all-reduce.4.cloned.1.call-update) | async-done | bytes 75280 | tf_op jit(solution)/shard_map/psum | solution.py:150
  582.2 1.5 broadcast_multiply_fusion.3
  (265 shorter events, 0.8 us)
Async XLA Ops:
  7.2 74.4 %all-gather.3.cloned.1.call-start = ((), (), s32[]{:S(2)}) async-start(), calls=%async_computation.2 | async-start | bytes 1253376 | tf_op jit(solution)/shard_map/all_gather | solution.py:83
  7.9 142.7 %all-gather.5.cloned.1.call-start = ((), (), s32[]{:S(2)}) async-start(), calls=%async_computation.3 | async-start | bytes 1253376 | tf_op jit(solution)/shard_map/all_gather | solution.py:84
  12.1 9.7 %collective-permute-start = (bf16[32,3,384]{2,1,0:T(4,128)(2,1)S(1)}, bf16[32,3,384]{2,1,0:T(4,128)(2,1)S(1)}, u32[]{:S(2)}, u32[]{:S(2)}) collective-permute-start(bf16[32,3,384]{2,1,0:T(4,128)(2,1)S(1)} %get-tuple-element.119), channel_id=1, source_target_pairs={{0,1},{1,2},{2,3},{3,4},{4,5},{5,6},{6,7},{7,8},{8,9},{9,10},{10,1... | collective-permute-start | bytes 221192 | tf_op jit(solution)/shard_map/ppermute | solution.py:20
  14.1 7.7 %collective-permute-start.1 = (bf16[32,3,384]{2,1,0:T(4,128)(2,1)S(1)}, bf16[32,3,384]{2,1,0:T(4,128)(2,1)S(1)}, u32[]{:S(2)}, u32[]{:S(2)}) collective-permute-start(bf16[32,3,384]{2,1,0:T(4,128)(2,1)S(1)} %get-tuple-element.120), channel_id=1, source_target_pairs={{1,0},{2,1},{3,2},{4,3},{5,4},{6,5},{7,6},{8,7},{9,8},{10,9},{11,1... | collective-permute-start | bytes 221192 | tf_op jit(solution)/shard_map/ppermute | solution.py:21
  18.0 215.1 %reduce-scatter.5.cloned.1.call-start = ((), (), s32[]{:S(2)}) async-start(), calls=%async_computation.5 | async-start | bytes 2506752 | tf_op jit(solution)/shard_map/reduce_scatter | solution.py:153
  22.5 3.1 collective-permute-start.2
  24.1 17.9 %copy-start.79 = (f32[384]{0:T(512)}, f32[384]{0:T(512)S(1)}, u32[]{:S(2)}) copy-start(f32[384]{0:T(512)S(1)} %get-tuple-element.94) | copy-start | bytes 4612
  24.1 17.9 %copy-start.81 = (f32[384]{0:T(512)}, f32[384]{0:T(512)S(1)}, u32[]{:S(2)}) copy-start(f32[384]{0:T(512)S(1)} %get-tuple-element.95) | copy-start | bytes 4612
  24.1 17.9 %copy-start.83 = (f32[384]{0:T(512)}, f32[384]{0:T(512)S(1)}, u32[]{:S(2)}) copy-start(f32[384]{0:T(512)S(1)} %get-tuple-element.96) | copy-start | bytes 4612
  24.1 17.9 %copy-start.84 = (f32[384]{0:T(512)}, f32[384]{0:T(512)S(1)}, u32[]{:S(2)}) copy-start(f32[384]{0:T(512)S(1)} %get-tuple-element.97) | copy-start | bytes 4612
  24.1 17.9 %copy-start.85 = (f32[384]{0:T(512)}, f32[384]{0:T(512)S(1)}, u32[]{:S(2)}) copy-start(f32[384]{0:T(512)S(1)} %get-tuple-element.98) | copy-start | bytes 4612
  24.1 17.9 %copy-start.86 = (f32[384]{0:T(512)}, f32[384]{0:T(512)S(1)}, u32[]{:S(2)}) copy-start(f32[384]{0:T(512)S(1)} %get-tuple-element.99) | copy-start | bytes 4612
  24.1 17.9 %copy-start.87 = (f32[384]{0:T(512)}, f32[384]{0:T(512)S(1)}, u32[]{:S(2)}) copy-start(f32[384]{0:T(512)S(1)} %get-tuple-element.100) | copy-start | bytes 4612
  24.1 17.9 %copy-start.88 = (f32[384]{0:T(512)}, f32[384]{0:T(512)S(1)}, u32[]{:S(2)}) copy-start(f32[384]{0:T(512)S(1)} %get-tuple-element.101) | copy-start | bytes 4612
  24.1 17.9 %copy-start.89 = (f32[384]{0:T(512)}, f32[384]{0:T(512)S(1)}, u32[]{:S(2)}) copy-start(f32[384]{0:T(512)S(1)} %get-tuple-element.102) | copy-start | bytes 4612
  24.2 5.8 collective-permute-start.3
  44.0 106.6 %copy-start.2 = (bf16[32,32,384]{2,1,0:T(8,128)(2,1)S(1)}, bf16[32,32,384]{2,1,0:T(8,128)(2,1)}, u32[]{:S(2)}) copy-start(bf16[32,32,384]{2,1,0:T(8,128)(2,1)} %param.12) | copy-start | bytes 2359300
  160.2 146.3 %reduce-scatter.3.cloned.1.call-start = ((), (), s32[]{:S(2)}) async-start(), calls=%async_computation.4 | async-start | bytes 2506752 | tf_op jit(solution)/shard_map/reduce_scatter | solution.py:152
  172.2 278.1 %all-reduce.6.cloned.1.call-start = ((), (), s32[]{:S(2)}) async-start(), calls=%async_computation.7 | async-start | bytes 761856 | tf_op jit(solution)/shard_map/psum | solution.py:155
  182.1 8.1 %collective-permute-start.4 = (bf16[32,3,384]{2,1,0:T(4,128)(2,1)S(1)}, bf16[32,3,384]{2,1,0:T(4,128)(2,1)S(1)}, u32[]{:S(2)}, u32[]{:S(2)}) collective-permute-start(bf16[32,3,384]{2,1,0:T(4,128)(2,1)S(1)} %get-tuple-element.117), channel_id=1, source_target_pairs={{0,1},{1,2},{2,3},{3,4},{4,5},{5,6},{6,7},{7,8},{8,9},{9,10},{10,1... | collective-permute-start | bytes 221192 | tf_op jit(solution)/shard_map/ppermute | solution.py:20
  182.8 7.4 %collective-permute-start.5 = (bf16[32,3,384]{2,1,0:T(4,128)(2,1)S(1)}, bf16[32,3,384]{2,1,0:T(4,128)(2,1)S(1)}, u32[]{:S(2)}, u32[]{:S(2)}) collective-permute-start(bf16[32,3,384]{2,1,0:T(4,128)(2,1)S(1)} %get-tuple-element.118), channel_id=1, source_target_pairs={{1,0},{2,1},{3,2},{4,3},{5,4},{6,5},{7,6},{8,7},{9,8},{10,9},{11,1... | collective-permute-start | bytes 221192 | tf_op jit(solution)/shard_map/ppermute | solution.py:21
  190.8 7.5 %collective-permute-start.6 = (bf16[3,38,384]{2,1,0:T(8,128)(2,1)S(1)}, bf16[3,38,384]{2,1,0:T(8,128)(2,1)S(1)}, u32[]{:S(2)}, u32[]{:S(2)}) collective-permute-start(bf16[3,38,384]{2,1,0:T(8,128)(2,1)S(1)} %get-tuple-element.114), channel_id=1, source_target_pairs={{0,16},{16,32},{32,48},{48,64},{64,80},{80,96},{96,112},{112,128},... | collective-permute-start | bytes 262664 | tf_op jit(solution)/shard_map/ppermute | solution.py:29
  195.5 111.1 %copy-start.1 = (bf16[32,32,384]{2,1,0:T(8,128)(2,1)S(1)}, bf16[32,32,384]{2,1,0:T(8,128)(2,1)}, u32[]{:S(2)}) copy-start(bf16[32,32,384]{2,1,0:T(8,128)(2,1)} %param.23) | copy-start | bytes 2359300
  195.5 111.1 %copy-start.6 = (f32[384]{0:T(512)S(1)}, f32[384]{0:T(512)}, u32[]{:S(2)}) copy-start(f32[384]{0:T(512)} %copy-done.5) | copy-start | bytes 4612
  195.5 111.1 %copy-start.8 = (f32[384]{0:T(512)S(1)}, f32[384]{0:T(512)}, u32[]{:S(2)}) copy-start(f32[384]{0:T(512)} %copy-done.7) | copy-start | bytes 4612
  195.5 111.1 %copy-start.10 = (f32[384]{0:T(512)S(1)}, f32[384]{0:T(512)}, u32[]{:S(2)}) copy-start(f32[384]{0:T(512)} %get-tuple-element.78) | copy-start | bytes 4612
  195.5 111.1 %copy-start.12 = (f32[384]{0:T(512)S(1)}, f32[384]{0:T(512)}, u32[]{:S(2)}) copy-start(f32[384]{0:T(512)} %get-tuple-element.79) | copy-start | bytes 4612
  195.6 111.1 %copy-start.14 = (f32[384]{0:T(512)S(1)}, f32[384]{0:T(512)}, u32[]{:S(2)}) copy-start(f32[384]{0:T(512)} %get-tuple-element.80) | copy-start | bytes 4612
  195.6 111.1 %copy-start.16 = (f32[384]{0:T(512)S(1)}, f32[384]{0:T(512)}, u32[]{:S(2)}) copy-start(f32[384]{0:T(512)} %get-tuple-element.81) | copy-start | bytes 4612
  195.6 111.1 %copy-start.18 = (f32[384]{0:T(512)S(1)}, f32[384]{0:T(512)}, u32[]{:S(2)}) copy-start(f32[384]{0:T(512)} %get-tuple-element.82) | copy-start | bytes 4612
  195.6 111.1 %copy-start.20 = (f32[384]{0:T(512)S(1)}, f32[384]{0:T(512)}, u32[]{:S(2)}) copy-start(f32[384]{0:T(512)} %get-tuple-element.83) | copy-start | bytes 4612
  195.6 111.1 %copy-start.22 = (f32[384]{0:T(512)S(1)}, f32[384]{0:T(512)}, u32[]{:S(2)}) copy-start(f32[384]{0:T(512)} %get-tuple-element.84) | copy-start | bytes 4612
  195.6 111.1 %copy-start.24 = (f32[384]{0:T(512)S(1)}, f32[384]{0:T(512)}, u32[]{:S(2)}) copy-start(f32[384]{0:T(512)} %get-tuple-element.85) | copy-start | bytes 4612
  195.6 111.1 %copy-start.26 = (f32[384]{0:T(512)S(1)}, f32[384]{0:T(512)}, u32[]{:S(2)}) copy-start(f32[384]{0:T(512)} %get-tuple-element.86) | copy-start | bytes 4612
  195.6 111.1 %copy-start.28 = (f32[384]{0:T(512)S(1)}, f32[384]{0:T(512)}, u32[]{:S(2)}) copy-start(f32[384]{0:T(512)} %get-tuple-element.87) | copy-start | bytes 4612
  195.6 111.1 %copy-start.30 = (f32[384]{0:T(512)S(1)}, f32[384]{0:T(512)}, u32[]{:S(2)}) copy-start(f32[384]{0:T(512)} %get-tuple-element.88) | copy-start | bytes 4612
  195.6 111.1 %copy-start.32 = (f32[384]{0:T(512)S(1)}, f32[384]{0:T(512)}, u32[]{:S(2)}) copy-start(f32[384]{0:T(512)} %get-tuple-element.89) | copy-start | bytes 4612
  195.7 111.1 %copy-start.34 = (f32[384]{0:T(512)S(1)}, f32[384]{0:T(512)}, u32[]{:S(2)}) copy-start(f32[384]{0:T(512)} %get-tuple-element.90) | copy-start | bytes 4612
  195.7 111.1 %copy-start.36 = (f32[384]{0:T(512)S(1)}, f32[384]{0:T(512)}, u32[]{:S(2)}) copy-start(f32[384]{0:T(512)} %get-tuple-element.91) | copy-start | bytes 4612
  195.7 111.1 %copy-start.38 = (f32[384]{0:T(512)S(1)}, f32[384]{0:T(512)}, u32[]{:S(2)}) copy-start(f32[384]{0:T(512)} %get-tuple-element.92) | copy-start | bytes 4612
  195.7 111.1 %copy-start.40 = (f32[384]{0:T(512)S(1)}, f32[384]{0:T(512)}, u32[]{:S(2)}) copy-start(f32[384]{0:T(512)} %get-tuple-element.93) | copy-start | bytes 4612
  195.7 111.1 %copy-start.42 = (f32[384]{0:T(512)S(1)}, f32[384]{0:T(512)}, u32[]{:S(2)}) copy-start(f32[384]{0:T(512)} %copy-done.41) | copy-start | bytes 4612
  195.7 111.1 %copy-start.44 = (f32[384]{0:T(512)S(1)}, f32[384]{0:T(512)}, u32[]{:S(2)}) copy-start(f32[384]{0:T(512)} %copy-done.43) | copy-start | bytes 4612
  195.7 111.1 %copy-start.46 = (f32[384]{0:T(512)S(1)}, f32[384]{0:T(512)}, u32[]{:S(2)}) copy-start(f32[384]{0:T(512)} %copy-done.45) | copy-start | bytes 4612
  195.7 111.1 %copy-start.48 = (f32[384]{0:T(512)S(1)}, f32[384]{0:T(512)}, u32[]{:S(2)}) copy-start(f32[384]{0:T(512)} %copy-done.47) | copy-start | bytes 4612
  195.7 111.1 %copy-start.50 = (f32[384]{0:T(512)S(1)}, f32[384]{0:T(512)}, u32[]{:S(2)}) copy-start(f32[384]{0:T(512)} %copy-done.49) | copy-start | bytes 4612
  195.7 111.1 %copy-start.52 = (f32[384]{0:T(512)S(1)}, f32[384]{0:T(512)}, u32[]{:S(2)}) copy-start(f32[384]{0:T(512)} %copy-done.51) | copy-start | bytes 4612
  195.8 111.1 %copy-start.54 = (f32[384]{0:T(512)S(1)}, f32[384]{0:T(512)}, u32[]{:S(2)}) copy-start(f32[384]{0:T(512)} %copy-done.53) | copy-start | bytes 4612
  195.8 111.1 %copy-start.56 = (f32[384]{0:T(512)S(1)}, f32[384]{0:T(512)}, u32[]{:S(2)}) copy-start(f32[384]{0:T(512)} %copy-done.55) | copy-start | bytes 4612
  195.8 111.1 %copy-start.58 = (f32[384]{0:T(512)S(1)}, f32[384]{0:T(512)}, u32[]{:S(2)}) copy-start(f32[384]{0:T(512)} %copy-done.57) | copy-start | bytes 4612
  195.8 111.1 %copy-start.60 = (f32[384]{0:T(512)S(1)}, f32[384]{0:T(512)}, u32[]{:S(2)}) copy-start(f32[384]{0:T(512)} %copy-done.59) | copy-start | bytes 4612
  195.8 111.1 %copy-start.62 = (f32[384]{0:T(512)S(1)}, f32[384]{0:T(512)}, u32[]{:S(2)}) copy-start(f32[384]{0:T(512)} %copy-done.61) | copy-start | bytes 4612
  195.8 111.1 %copy-start.64 = (f32[384]{0:T(512)S(1)}, f32[384]{0:T(512)}, u32[]{:S(2)}) copy-start(f32[384]{0:T(512)} %copy-done.63) | copy-start | bytes 4612
  195.8 111.1 %copy-start.66 = (f32[384]{0:T(512)S(1)}, f32[384]{0:T(512)}, u32[]{:S(2)}) copy-start(f32[384]{0:T(512)} %copy-done.65) | copy-start | bytes 4612
  195.8 111.1 %copy-start.68 = (f32[384]{0:T(512)S(1)}, f32[384]{0:T(512)}, u32[]{:S(2)}) copy-start(f32[384]{0:T(512)} %copy-done.67) | copy-start | bytes 4612
  195.8 111.1 %copy-start.70 = (f32[384]{0:T(512)S(1)}, f32[384]{0:T(512)}, u32[]{:S(2)}) copy-start(f32[384]{0:T(512)} %copy-done.69) | copy-start | bytes 4612
  195.8 111.1 %copy-start.72 = (f32[384]{0:T(512)S(1)}, f32[384]{0:T(512)}, u32[]{:S(2)}) copy-start(f32[384]{0:T(512)} %copy-done.71) | copy-start | bytes 4612
  195.9 111.1 %copy-start.74 = (f32[384]{0:T(512)S(1)}, f32[384]{0:T(512)}, u32[]{:S(2)}) copy-start(f32[384]{0:T(512)} %copy-done.73) | copy-start | bytes 4612
  195.9 111.1 %copy-start.76 = (f32[384]{0:T(512)S(1)}, f32[384]{0:T(512)}, u32[]{:S(2)}) copy-start(f32[384]{0:T(512)} %copy-done.75) | copy-start | bytes 4612
  195.9 111.1 %copy-start.78 = (f32[384]{0:T(512)S(1)}, f32[384]{0:T(512)}, u32[]{:S(2)}) copy-start(f32[384]{0:T(512)} %copy-done.77) | copy-start | bytes 4612
  195.9 111.1 %copy-start.80 = (f32[384]{0:T(512)S(1)}, f32[384]{0:T(512)}, u32[]{:S(2)}) copy-start(f32[384]{0:T(512)} %copy-done.79) | copy-start | bytes 4612
  195.9 111.1 %copy-start.82 = (f32[384]{0:T(512)S(1)}, f32[384]{0:T(512)}, u32[]{:S(2)}) copy-start(f32[384]{0:T(512)} %copy-done.81) | copy-start | bytes 4612
  196.8 5.7 collective-permute-start.7
  306.6 275.6 %all-reduce.4.cloned.1.call-start = ((), (), s32[]{:S(2)}) async-start(), calls=%async_computation.6 | async-start | bytes 172032 | tf_op jit(solution)/shard_map/psum | solution.py:150
  (51 other events, 383.9 us)
Sparse Core Ops, SparseCore 0:
  9.8 71.7 all-gather.2
  83.4 67.1 all-gather.4
  160.3 72.7 reduce-scatter.4
  235.5 71.0 reduce-scatter.2
  309.8 140.3 all-reduce.5
  452.9 129.2 all-reduce.3
